TPU v7x, 256 devices: a whole 4x4x8 slice. The times are simulated.
256 devices in a mesh: row: 64 (over z_hi, y, x), rep: 4 (over z_lo, core).
Axes of the slice: x: 4, y: 4, z: 8 (z_hi: 4, z_lo: 2; z = z_hi * 2 + z_lo), core: 2. Of those that a mesh axis runs over, the one named last changes fastest.
Arguments:
- features: bfloat16 [32768, 128], P('row'), may hold values from -6 to 6
- weight_one: bfloat16 [128, 128], replicated, may hold values from -0.5 to 0.5
- weight_two: bfloat16 [128, 128], replicated, may hold values from -0.5 to 0.5
- cotangent: bfloat16 [32768, 128], P('row'), may hold values from -0.03125 to 0.03125
- adj_tiles: bfloat16 [64, 64, 16, 128, 128], P('row', 'rep'), may hold values from -0.09375 to 0.09375
- tile_rows: int32 [64, 64, 16], P('row', 'rep'), may hold values from 0 to 3, as said below
- tile_cols: int32 [64, 64, 16], P('row', 'rep'), may hold values from 0 to 3
- tile_counts: int32 [64, 64], P('row', 'rep'), may hold values from 0 to 16, as said below
Outputs:
- output: bfloat16 [32768, 128], P('row')
- grad_one: float32 [128, 128], replicated
- grad_two: float32 [128, 128], replicated
Inputs may be any that keep to these rules, and one draw needn't show every extreme that they name: Only slots 0 to tile_counts[b, s] - 1 of block-row b and section s are live; the other slots carry arbitrary tiles and indices that are not part of A. Section b of block-row b holds 16 live slots; many other sections hold none. `tile_rows`: the (row, column) pairs of the slots of one block-row and section are distinct.
All inputs are finite; a program needn't handle non-finite values.
Results may differ from a plain program's by a relative error of at most 0.0065.
Values may be sent and summed in bfloat16 or wider, within the bound.
A program may use at most 192 MiB of HBM per device.

v0:
```python
from functools import partial

import jax
import jax.numpy as jnp
from jax import lax
from jax.sharding import PartitionSpec as P

TILE = 128


def gelu_value(values):
    return values * 0.5 * (1.0 + lax.erf(values * 0.7071067811865476))


def gelu_slope(values):
    normal_cdf = 0.5 * (1.0 + lax.erf(values * 0.7071067811865476))
    return normal_cdf + values * jnp.exp(-0.5 * values * values) * 0.3989422804014327


def row_contract(left, right):
    return lax.dot_general(
        left, right, (((0,), (0,)), ((), ())), preferred_element_type=jnp.float32
    )


def section_work(running, pieces, section_tiles, section_rows, section_cols, live_count):
    slot_total = section_tiles.shape[0]
    count_tiles = running.shape[0]
    sources = jnp.take(pieces, section_cols, axis=0)
    products = jnp.einsum(
        "mij,mjf->mif", section_tiles, sources, preferred_element_type=jnp.float32
    )
    live_mask = jnp.arange(slot_total, dtype=jnp.int32) < live_count
    onehot = jnp.where(
        live_mask[:, None]
        & (section_rows[:, None] == jnp.arange(count_tiles, dtype=jnp.int32)[None, :]),
        1.0,
        0.0,
    ).astype(jnp.float32)
    return running + jnp.einsum("mk,mif->kif", onehot, products, precision=lax.Precision.HIGHEST)


def propagate(tile_data, row_ids, col_ids, live_counts, own_block):
    section_total = tile_data.shape[0]
    block_rows = own_block.shape[0]
    count_tiles = block_rows // TILE
    width = own_block.shape[1]
    first_section = lax.axis_index("rep") * section_total

    def pick(section_id):
        return (
            lax.dynamic_index_in_dim(tile_data, section_id, 0, keepdims=False),
            lax.dynamic_index_in_dim(row_ids, section_id, 0, keepdims=False),
            lax.dynamic_index_in_dim(col_ids, section_id, 0, keepdims=False),
            lax.dynamic_index_in_dim(live_counts, section_id, 0, keepdims=False),
        )

    zeros = jnp.zeros((count_tiles, TILE, width), jnp.float32)
    kept_total = section_total * block_rows
    kept_base = first_section * block_rows
    empty = jnp.zeros((kept_total, width), own_block.dtype)
    piece = lax.all_gather(own_block, "row", axis=0, tiled=True)
    piece_rows = piece.shape[0]
    padding = jnp.zeros((piece_rows, width), empty.dtype)
    widened = jnp.concatenate([padding, empty, padding], axis=0)
    offset = jnp.clip(jnp.int32(0) - kept_base + piece_rows, 0, kept_total + piece_rows)
    widened = lax.dynamic_update_slice_in_dim(widened, piece, offset, 0)
    kept = widened[piece_rows : piece_rows + kept_total]
    kept = kept.reshape(section_total, count_tiles, TILE, width)

    def kept_step(section_id, running):
        pieces = lax.dynamic_index_in_dim(kept, section_id, 0, keepdims=False)
        return section_work(running, pieces, *pick(section_id))

    summed = lax.fori_loop(0, section_total, kept_step, zeros)
    return summed.reshape(block_rows, width)


def whole_sum(partial_rows):
    return lax.psum(partial_rows, "rep")


def per_device(
    features, weight_one, weight_two, cotangent, adj_tiles, tile_rows, tile_cols, tile_counts
):
    spread = partial(propagate, adj_tiles[0], tile_rows[0], tile_cols[0], tile_counts[0])
    d_two = lax.dot_general(
        cotangent, weight_two, (((1,), (1,)), ((), ())), preferred_element_type=jnp.float32
    ).astype(jnp.bfloat16)
    s_one = whole_sum(spread(features)).astype(jnp.bfloat16)
    pre_one = jnp.dot(s_one, weight_one, preferred_element_type=jnp.float32)
    hidden = gelu_value(pre_one).astype(jnp.bfloat16)
    s_two = whole_sum(spread(hidden)).astype(jnp.bfloat16)
    output = jnp.dot(s_two, weight_two, preferred_element_type=jnp.float32).astype(jnp.bfloat16)
    grad_two = lax.psum(row_contract(s_two, cotangent), "row")
    d_hidden = whole_sum(spread(d_two))
    d_pre = (d_hidden * gelu_slope(pre_one)).astype(jnp.bfloat16)
    grad_one = lax.psum(row_contract(s_one, d_pre), "row")
    return (output, grad_one, grad_two)


def solution(mesh):
    placed = (
        P("row", None),
        P(),
        P(),
        P("row", None),
        P("row", "rep", None, None, None),
        P("row", "rep", None),
        P("row", "rep", None),
        P("row", "rep"),
    )
    return jax.shard_map(
        per_device,
        mesh=mesh,
        in_specs=placed,
        out_specs=(P("row", None), P(), P()),
        check_vma=False,
    )
```

profile of v0, /device:TPU:1, one launch (start us, length us, event | category | flops | bytes accessed | tf_op | source)
XLA Modules:
  0.0 1345.8 jit_solution(14181095154365439595)
XLA Ops:
  8.1 1.6 convolution_convert_fusion
  10.6 3.9 broadcast.50
  14.4 15.8 %pad_maximum_fusion = bf16[73728,128]{1,0:T(8,128)(2,1)S(1)} fusion(bf16[32768,128]{1,0:T(8,128)(2,1)} %broadcast.50, bf16[73728]{0:T(1024)(128)(2,1)S(1)} %pad.1.clone), kind=kLoop, calls=%fused_computation.90 | loop fusion | flops 56623104 | bytes 27410432 | tf_op jit(solution)/shard_map/concatenate | solution.py:65
  30.2 6.4 copy.46
  36.6 5.8 copy-done.1
  42.4 6.5 copy.38
  48.8 74.7 %all-gather.8.cloned.1.call-done = bf16[32768,128]{1,0:T(8,128)(2,1)} async-done(((bf16[512,128]{1,0:T(8,128)(2,1)}), bf16[32768,128]{1,0:T(8,128)(2,1)}) %all-gather.8.cloned.1.call-update) | async-done | bytes 8388624 | tf_op jit(solution)/shard_map/all_gather | solution.py:62
  123.5 39.1 %dynamic_update_slice.11 = bf16[73728,128]{1,0:T(8,128)(2,1)} dynamic-update-slice(bf16[73728,128]{1,0:T(8,128)(2,1)} %copy.46, bf16[32768,128]{1,0:T(8,128)(2,1)} %all-gather.8.cloned.1.call-done, s32[]{:T(128)S(6)} %min.6, s32[]{:T(128)} %constant.163.clone.1) | dynamic-update-slice | bytes 16777220 | tf_op jit(solution)/shard_map/dynamic_update_slice | solution.py:67
  162.6 3.0 slice.20
  165.6 113.0 %while.44 = (s32[]{:T(128)}, f32[4,128,128]{2,0,1:T(4,128)S(1)}, s32[16]{0:T(128)S(1)}, s32[16,16]{1,0:T(8,128)}, bf16[16,16,128,128]{3,2,1,0:T(8,128)(2,1)}, /*...) while((s32[]{:T(128)}, f32[4,128,128]{2,0,1:T(4,128)S(1)}, ...), condition=%wide.region_7.9_spmd.clone, body=%wide.region_6.8_spmd.clone.sunk | while | flops 80086320 | bytes 4985487 | solution.py:75
  205.2 1.5 fusion.124
  279.5 39.1 %dynamic_update_slice.9 = bf16[73728,128]{1,0:T(8,128)(2,1)} dynamic-update-slice(bf16[73728,128]{1,0:T(8,128)(2,1)} %copy-done.1, bf16[32768,128]{1,0:T(8,128)(2,1)} %all-gather.4.cloned.1.call-done, s32[]{:T(128)S(6)} %min.6, s32[]{:T(128)} %constant.163.clone.1) | dynamic-update-slice | bytes 16777220 | tf_op jit(solution)/shard_map/dynamic_update_slice | solution.py:67
  318.6 1.7 slice.18
  320.4 98.5 %while.42 = (s32[]{:T(128)}, f32[4,128,128]{2,0,1:T(4,128)S(1)}, s32[16]{0:T(128)S(1)}, s32[16,16]{1,0:T(8,128)}, bf16[16,16,128,128]{3,2,1,0:T(8,128)(2,1)}, /*...) while((s32[]{:T(128)}, f32[4,128,128]{2,0,1:T(4,128)S(1)}, ...), condition=%wide.region_1.3_spmd.clone, body=%wide.region_0.2_spmd.clone.sunk | while | flops 80086320 | bytes 4985487 | solution.py:75
  418.9 19.8 %all-reduce.9 = bf16[512,128]{1,0:T(8,128)(2,1)S(1)} all-reduce(f32[512,128]{1,0:T(8,128)S(1)} %bitcast.102), channel_id=1, replica_groups=mesh['row'=64,'rep'=4] {'rep'}, use_global_device_ids=true, to_apply=%region_2.4 | all-reduce | flops 65536 | bytes 393216 | tf_op jit(solution)/shard_map/psum | solution.py:80
  439.7 1.9 fusion.69
  441.5 105.7 %all-gather.6.cloned.1.call-done = bf16[32768,128]{1,0:T(8,128)(2,1)} async-done(((bf16[512,128]{1,0:T(8,128)(2,1)}), bf16[32768,128]{1,0:T(8,128)(2,1)}) %all-gather.6.cloned.1.call-update) | async-done | bytes 8388624 | tf_op jit(solution)/shard_map/all_gather | solution.py:62
  547.3 39.1 %dynamic_update_slice.10 = bf16[73728,128]{1,0:T(8,128)(2,1)} dynamic-update-slice(bf16[73728,128]{1,0:T(8,128)(2,1)} %copy.38, bf16[32768,128]{1,0:T(8,128)(2,1)} %all-gather.6.cloned.1.call-done, s32[]{:T(128)S(6)} %min.6, s32[]{:T(128)} %constant.163.clone.1) | dynamic-update-slice | bytes 16777220 | tf_op jit(solution)/shard_map/dynamic_update_slice | solution.py:67
  586.4 1.7 slice.19
  588.1 98.5 %while.43 = (s32[]{:T(128)}, f32[4,128,128]{2,0,1:T(4,128)S(1)}, s32[16]{0:T(128)S(1)}, s32[16,16]{1,0:T(8,128)}, bf16[16,16,128,128]{3,2,1,0:T(8,128)(2,1)}, /*...) while((s32[]{:T(128)}, f32[4,128,128]{2,0,1:T(4,128)S(1)}, ...), condition=%wide.region_4.6_spmd.clone, body=%wide.region_3.5_spmd.clone.sunk | while | flops 80086320 | bytes 4985487 | solution.py:75
  686.6 19.9 %all-reduce.10 = bf16[512,128]{1,0:T(8,128)(2,1)S(1)} all-reduce(f32[512,128]{1,0:T(8,128)S(1)} %bitcast.103), channel_id=1, replica_groups=mesh['row'=64,'rep'=4] {'rep'}, use_global_device_ids=true, to_apply=%region_5.7 | all-reduce | flops 65536 | bytes 393216 | tf_op jit(solution)/shard_map/psum | solution.py:80
  708.3 628.0 %all-reduce.8.cloned.1.call-done = (f32[128,128]{1,0:T(8,128)}, f32[128,128]{1,0:T(8,128)}) async-done(((f32[128,128]{1,0:T(8,128)}, f32[128,128]{1,0:T(8,128)}), (f32[128,128]{1,0:T(8,128)}, f32[128,128]{1,0:T(8,128)})) %all-reduce.8.cloned.1.call-update) | async-done | bytes 131088 | tf_op jit(solution)/shard_map/psum | solution.py:98
  1336.3 1.5 copy.58
  1337.8 1.5 copy.59
  (465 shorter events, 311.5 us)
Async XLA Ops:
  7.2 0.9 copy-start
  7.2 116.4 %all-gather.8.cloned.1.call-start = ((), (), s32[]{:S(2)}) async-start(), calls=%async_computation.2 | async-start | bytes 8519680 | tf_op jit(solution)/shard_map/all_gather | solution.py:62
  9.7 269.8 %all-gather.4.cloned.1.call-start = ((), (), s32[]{:S(2)}) async-start(), calls=%async_computation | async-start | bytes 8519680 | tf_op jit(solution)/shard_map/all_gather | solution.py:62
  10.5 429.2 %all-reduce.6.cloned.1.call-start = ((), (), s32[]{:S(2)}) async-start(), calls=%async_computation.3 | async-start | bytes 524288 | tf_op jit(solution)/shard_map/psum | solution.py:80
  30.2 12.2 copy-start.1
  48.8 116.8 %copy-start.2 = (f32[4,128,128]{2,0,1:T(4,128)S(1)}, f32[4,128,128]{2,0,1:T(4,128)}, u32[]{:S(2)}) copy-start(f32[4,128,128]{2,0,1:T(4,128)} %custom-call.2) | copy-start | bytes 786436
  48.8 116.8 %copy-start.5 = (s32[1,16]{1,0:T(1,128)S(1)}, s32[1,16]{1,0:T(1,128)}, u32[]{:S(2)}) copy-start(s32[1,16]{1,0:T(1,128)} %param.23) | copy-start | bytes 196
  279.4 267.8 %all-gather.6.cloned.1.call-start = ((), (), s32[]{:S(2)}) async-start(), calls=%async_computation.1 | async-start | bytes 8519680 | tf_op jit(solution)/shard_map/all_gather | solution.py:62
  320.3 118.3 %copy-start.4 = (bf16[128,128]{1,0:T(8,128)(2,1)S(1)}, bf16[128,128]{1,0:T(8,128)(2,1)}, u32[]{:S(2)}) copy-start(bf16[128,128]{1,0:T(8,128)(2,1)} %param.17) | copy-start | bytes 98308
  439.6 896.7 %all-reduce.8.cloned.1.call-start = ((), (), s32[]{:S(2)}) async-start(), calls=%async_computation.4 | async-start | bytes 262144 | tf_op jit(solution)/shard_map/psum | solution.py:98
  588.1 119.3 %copy-start.3 = (bf16[128,128]{1,0:T(8,128)(2,1)S(1)}, bf16[128,128]{1,0:T(8,128)(2,1)}, u32[]{:S(2)}) copy-start(bf16[128,128]{1,0:T(8,128)(2,1)} %param.18) | copy-start | bytes 98308
Sparse Core Ops, SparseCore 0:
  11.9 111.5 all-gather.7
  126.8 113.1 all-gather.3
  279.6 46.4 all-reduce.5
  439.7 107.5 all-gather.5
  707.6 628.6 all-reduce.7
where the time goes:
time: 1370 us; the launch traced here: 1350 us
  waiting for transfers between devices  809 us (59%)
  local copies, waits for them, and re-layouts  259 us (19%)
  matrix products  141 us (10%)
  other arithmetic  80.6 us (6%)
  blocking collectives  39.7 us (3%)
  between operations  14 us (1%)
    psum x1, waiting for transfers between devices, per_device(): grad_one = lax.psum(row_contract(s_one, d_pre), 'row')  628 us
    all_gather x3, waiting for transfers between devices, propagate(): piece = lax.all_gather(own_block, 'row', axis=0, tiled=True)  180 us
    dynamic_update_slice x3, local copies, waits for them, and re-layouts, propagate(): widened = lax.dynamic_update_slice_in_dim(widened, piece, offset, 0)  117 us
    dot_general x48, matrix products, section_work(): jnp.einsum('mij,mjf->mif', section_tiles, sources, preferred_element_type...  68.1 us
    dot_general x48, matrix products, section_work(): jnp.einsum('mk,mif->kif', onehot, products, precision=lax.Precision.HIGHEST)  66.7 us
    psum x2, blocking collectives, whole_sum(): return lax.psum(partial_rows, 'rep')  39.7 us
    eq x48, local copies, waits for them, and re-layouts, section_work(): section_rows[:, None] == jnp.arange(count_tiles, dtype=jnp.int32)[None, :]  33.5 us
    and x48, other arithmetic, section_work(): sources = jnp.take(pieces, section_cols, axis=0)  33.4 us
  transfers between devices with their start and end apart: 5, of which 3 were waited for; matrix products, arithmetic and copies ran while one was open for 25% of the time, Pallas kernels for 0%

commit v1 on v0

v1 whole, which is shorter than its diff:
```python
import jax
import jax.numpy as jnp
from jax import lax
from jax.experimental import pallas as pl
from jax.experimental.pallas import tpu as pltpu
from jax.sharding import PartitionSpec as P

MESH = pl.DeviceIdType.MESH
TILE = 128
NB = 512
HALF = 256
SIDE = 4
PLANE = 16
REPS = 4
DEAD = 256
BF16 = jnp.bfloat16
F32 = jnp.float32


def gelu_parts(values):
    normal_cdf = 0.5 * (1.0 + lax.erf(values * 0.7071067811865476))
    slope = normal_cdf + values * jnp.exp(-0.5 * values * values) * 0.3989422804014327
    return values * normal_cdf, slope


def wrap(value, size):
    return lax.rem(value + size, size)


def ring_step(index):
    return index + index // 2 - 2 * (index // 3)


def step_kernel(
    feat, w_one, w_two, cot, adj, rows_in, cols_in, counts_in,
    out, grad_one, grad_two,
    tiles, table_v, table_s, xf, xd, xh, dq, hq, acc_f, acc_d, acc_h,
    part_f, part_d, part_h, red_f, red_d, red_h, s_one_q, slope_q, out_buf,
    gpart, grs, gcol, gred, gall,
    local_sem, z_send, z_recv, a_send, a_recv, b_send, b_recv,
    r_send, r_recv, o_send, o_recv, g_send, g_recv,
):
    row = lax.axis_index("row")
    rep = lax.axis_index("rep")
    zh = row // PLANE
    place = lax.rem(row, PLANE)
    y = place // SIDE
    x = lax.rem(place, SIDE)
    column = zh * REPS + rep

    adj_copy = pltpu.make_async_copy(adj, tiles.at[pl.ds(0, DEAD)], local_sem.at[0])
    adj_copy.start()

    def plane_peer(step):
        return (zh * PLANE + wrap(place + step, PLANE), rep)

    def column_peer(step):
        other = wrap(column + step, PLANE)
        return ((other // REPS) * PLANE + place, lax.rem(other, REPS))

    def rep_peer(step):
        return (row, wrap(rep + step, REPS))

    def x_peer(step):
        return (zh * PLANE + y * SIDE + wrap(x + step, SIDE), rep)

    def y_peer(step):
        return (zh * PLANE + wrap(y + step, SIDE) * SIDE + x, rep)

    def remote(src, dst, send, recv, peer):
        return pltpu.make_async_remote_copy(
            src_ref=src, dst_ref=dst, send_sem=send, recv_sem=recv,
            device_id=peer, device_id_type=MESH,
        )

    barrier = pltpu.get_barrier_semaphore()

    def greet(step, carry):
        pl.semaphore_signal(barrier, inc=1, device_id=plane_peer(step), device_id_type=MESH)
        pl.semaphore_signal(barrier, inc=1, device_id=column_peer(step), device_id_type=MESH)
        return carry

    lax.fori_loop(1, PLANE, greet, 0)
    pl.semaphore_wait(barrier, 2 * (PLANE - 1))

    def z_copy(t, buf, src, step):
        return remote(
            src,
            buf.at[place, pl.ds(pl.multiple_of(rep * TILE, TILE), TILE)],
            z_send.at[t, step], z_recv.at[t, rep],
            (wrap(zh + step, REPS) * PLANE + place, zh),
        )

    def z_start(t, buf, src):
        for step in (1, 2, 3):
            z_copy(t, buf, src, step).start()

        @pl.when(rep != zh)
        def _():
            z_copy(t, buf, src, 0).start()

        @pl.when(rep == zh)
        def _():
            buf[place, pl.ds(pl.multiple_of(rep * TILE, TILE), TILE)] = src[...]

    def z_finish(t, buf, src):
        for step in (1, 2, 3):
            z_copy(t, buf, src, step).wait_send()

        @pl.when(rep != zh)
        def _():
            z_copy(t, buf, src, 0).wait_send()

    def z_wait(t, buf, src, quarter):
        @pl.when(jnp.logical_or(rep != zh, rep != quarter))
        def _():
            remote(
                src, buf.at[place, pl.ds(quarter * TILE, TILE)],
                z_send.at[t, 0], z_recv.at[t, quarter], rep_peer(1),
            ).wait_recv()

    def a_block(dy, dx):
        return wrap(y - dy, SIDE) * SIDE + wrap(x - dx, SIDE)

    def half_a(buf, block):
        return buf.at[block, pl.ds(0, HALF)]

    def half_b(buf, block):
        return buf.at[block, pl.ds(HALF, HALF)]

    def first_a(t, buf, i, block):
        return remote(half_a(buf, block), half_a(buf, block),
                      a_send.at[t, i], a_recv.at[t, i], x_peer(ring_step(i + 1)))

    def first_b(t, buf, i, block):
        return remote(half_b(buf, block), half_b(buf, block),
                      b_send.at[t, i], b_recv.at[t, i], y_peer(ring_step(i + 1)))

    def second_a(t, buf, j, i, block):
        return remote(half_a(buf, block), half_a(buf, block),
                      a_send.at[t, 3 + 4 * j + i], a_recv.at[t, 3 + 4 * j + i],
                      y_peer(ring_step(j + 1)))

    def second_b(t, buf, j, i, block):
        return remote(half_b(buf, block), half_b(buf, block),
                      b_send.at[t, 3 + 4 * j + i], b_recv.at[t, 3 + 4 * j + i],
                      x_peer(ring_step(j + 1)))

    def spread_start(t, buf, src):
        z_wait(t, buf, src, 0)
        z_wait(t, buf, src, 1)
        for i in range(3):
            first_a(t, buf, i, place).start()
        z_wait(t, buf, src, 2)
        z_wait(t, buf, src, 3)
        for i in range(3):
            first_b(t, buf, i, place).start()
        for j in range(3):
            second_a(t, buf, j, 0, place).start()
            second_b(t, buf, j, 0, place).start()

    def spread_forward(t, buf):
        def body(i, carry):
            away = ring_step(i + 1)
            from_x = a_block(0, away)
            first_a(t, buf, i, from_x).wait_recv()
            for j in range(3):
                second_a(t, buf, j, i + 1, from_x).start()
            from_y = a_block(away, 0)
            first_b(t, buf, i, from_y).wait_recv()
            for j in range(3):
                second_b(t, buf, j, i + 1, from_y).start()
            return carry

        lax.fori_loop(0, 3, body, 0)

    def spread_finish(t, buf):
        def body(i, carry):
            first_a(t, buf, i, place).wait_send()
            first_b(t, buf, i, place).wait_send()
            for j in range(4):
                second_a(t, buf, i, j, place).wait_send()
                second_b(t, buf, i, j, place).wait_send()
            return carry

        lax.fori_loop(0, 3, body, 0)

    def consume(buf, acc, block, half):
        right = buf[block, pl.ds(half * HALF, HALF)]
        for k in range(4):
            left = jnp.concatenate(
                [tiles[table_s[block, 4 * k + 2 * half]], tiles[table_s[block, 4 * k + 2 * half + 1]]],
                axis=1,
            )
            acc[pl.ds(k * TILE, TILE)] += jnp.dot(left, right, preferred_element_type=F32)

    def consume_near(buf, acc):
        def body(i, carry):
            away = ring_step(i)
            consume(buf, acc, a_block(0, away), 0)
            consume(buf, acc, a_block(away, 0), 1)
            return carry

        lax.fori_loop(0, 4, body, 0)

    def consume_far(t, buf, acc, start, stop):
        def body(n, carry):
            j = n // 4
            i = lax.rem(n, 4)
            e = ring_step(j + 1)
            d = ring_step(i)
            block = a_block(e, d)
            second_a(t, buf, j, i, block).wait_recv()
            consume(buf, acc, block, 0)
            block = a_block(d, e)
            second_b(t, buf, j, i, block).wait_recv()
            consume(buf, acc, block, 1)
            return carry

        lax.fori_loop(start, stop, body, 0)

    def rep_copy(t, part, red, step):
        return remote(
            part.at[pl.ds(pl.multiple_of(wrap(rep + step, REPS) * TILE, TILE), TILE)],
            red.at[step - 1], r_send.at[t, step - 1], r_recv.at[t, step - 1],
            rep_peer(step),
        )

    def rep_start(t, acc, part, red):
        part[...] = acc[...].astype(BF16)
        for step in (2, 3, 1):
            rep_copy(t, part, red, step).start()

    def rep_sum(t, acc, part, red):
        total = acc[pl.ds(pl.multiple_of(rep * TILE, TILE), TILE)]
        for step in (1, 2, 3):
            rep_copy(t, part, red, step).wait_recv()
            total = total + red[step - 1].astype(F32)
        return total

    quarter = pl.ds(pl.multiple_of(rep * TILE, TILE), TILE)

    fq = feat.at[quarter]
    z_start(0, xf, fq)
    dq[...] = lax.dot_general(
        cot[quarter], w_two[...], (((1,), (1,)), ((), ())), preferred_element_type=F32
    ).astype(BF16)
    z_start(1, xd, dq)

    lanes = lax.broadcasted_iota(jnp.int32, (PLANE, TILE), 1)
    sections = lax.broadcasted_iota(jnp.int32, (PLANE, TILE), 0)
    small_lane = lax.broadcasted_iota(jnp.int32, (PLANE, PLANE), 1)
    small_row = lax.broadcasted_iota(jnp.int32, (PLANE, PLANE), 0)
    count_wide = jnp.broadcast_to(counts_in[...].astype(F32), (PLANE, PLANE))
    count_col = jnp.sum(jnp.where(small_lane == small_row, count_wide, 0.0), axis=1, keepdims=True)
    cell = jnp.where(
        small_lane.astype(F32) < count_col, rows_in[...] * 4 + cols_in[...], -1
    )
    table = jnp.full((PLANE, TILE), DEAD, jnp.int32)
    for slot in range(16):
        table = jnp.where(cell[:, slot : slot + 1] == lanes, sections * 16 + slot, table)
    table_v[...] = table
    table_copy = pltpu.make_async_copy(table_v, table_s, local_sem.at[1])
    table_copy.start()
    tiles[DEAD] = jnp.zeros((TILE, TILE), BF16)
    acc_f[...] = jnp.zeros_like(acc_f)
    acc_d[...] = jnp.zeros_like(acc_d)
    acc_h[...] = jnp.zeros_like(acc_h)

    spread_start(0, xf, fq)
    table_copy.wait()
    adj_copy.wait()
    spread_forward(0, xf)
    consume_near(xf, acc_f)
    spread_start(1, xd, dq)
    consume_far(0, xf, acc_f, 0, 12)
    rep_start(0, acc_f, part_f, red_f)
    spread_forward(1, xd)

    s_one = rep_sum(0, acc_f, part_f, red_f).astype(BF16)
    pre_one = jnp.dot(s_one, w_one[...], preferred_element_type=F32)
    hidden, slope = gelu_parts(pre_one)
    hq[...] = hidden.astype(BF16)
    z_start(2, xh, hq)
    s_one_q[...] = s_one
    slope_q[...] = slope
    consume_near(xd, acc_d)
    spread_start(2, xh, hq)
    consume_far(1, xd, acc_d, 0, 12)
    rep_start(1, acc_d, part_d, red_d)
    spread_forward(2, xh)
    consume_near(xh, acc_h)
    d_pre = (rep_sum(1, acc_d, part_d, red_d) * slope_q[...]).astype(BF16)
    g_one = lax.dot_general(
        s_one_q[...], d_pre, (((0,), (0,)), ((), ())), preferred_element_type=F32
    )
    gpart[:, 0:8, :] = g_one.reshape(PLANE, 8, TILE)
    consume_far(2, xh, acc_h, 0, 12)
    rep_start(2, acc_h, part_h, red_h)

    g_two = lax.dot_general(
        part_h[...], cot[...], (((0,), (0,)), ((), ())), preferred_element_type=F32
    )
    gpart[:, 8:16, :] = g_two.reshape(PLANE, 8, TILE)

    def plane_sum(step):
        return remote(
            gpart.at[wrap(place + step, PLANE)], grs.at[step],
            g_send.at[0, step], g_recv.at[0, step], plane_peer(step),
        )

    def column_share(step):
        return remote(
            gcol.at[column], gcol.at[column],
            g_send.at[1, step], g_recv.at[1, step], column_peer(step),
        )

    def plane_gather(step):
        return remote(
            gred, gall.at[place],
            g_send.at[2, step], g_recv.at[2, step], plane_peer(step),
        )

    def start_all(make):
        def body(step, carry):
            make(step).start()
            return carry

        lax.fori_loop(1, PLANE, body, 0)

    def receive_all(make):
        def body(step, carry):
            make(step).wait_recv()
            return carry

        lax.fori_loop(1, PLANE, body, 0)

    def sent_all(make):
        def body(step, carry):
            make(step).wait_send()
            return carry

        lax.fori_loop(1, PLANE, body, 0)

    start_all(plane_sum)

    s_two = rep_sum(2, acc_h, part_h, red_h).astype(BF16)
    out_buf[quarter] = jnp.dot(s_two, w_two[...], preferred_element_type=F32).astype(BF16)

    def out_copy(step):
        return remote(
            out_buf.at[quarter], out_buf.at[quarter],
            o_send.at[step - 1], o_recv.at[step - 1], rep_peer(step),
        )

    for step in (2, 3, 1):
        out_copy(step).start()

    receive_all(plane_sum)
    mine = gpart[place]
    for step in range(1, PLANE):
        mine = mine + grs[step]
    gcol[column] = mine
    start_all(column_share)
    receive_all(column_share)
    mine = gcol[0]
    for other in range(1, PLANE):
        mine = mine + gcol[other]
    gred[...] = mine
    start_all(plane_gather)
    gall[place] = mine

    for step in (1, 2, 3):
        out_copy(step).wait_recv()
    out[...] = out_buf[...]
    receive_all(plane_gather)
    grad_one[...] = gall[:, 0:8, :].reshape(TILE, TILE)
    grad_two[...] = gall[:, 8:16, :].reshape(TILE, TILE)

    for t, buf, src in ((0, xf, fq), (1, xd, dq), (2, xh, hq)):
        z_finish(t, buf, src)
        spread_finish(t, buf)
    for t, part, red in ((0, part_f, red_f), (1, part_d, red_d), (2, part_h, red_h)):
        for step in (1, 2, 3):
            rep_copy(t, part, red, step).wait_send()
    for step in (1, 2, 3):
        out_copy(step).wait_send()
    sent_all(plane_sum)
    sent_all(column_share)
    sent_all(plane_gather)


def per_device(
    features, weight_one, weight_two, cotangent, adj_tiles, tile_rows, tile_cols, tile_counts
):
    vmem = pl.BlockSpec(memory_space=pltpu.VMEM)
    dma = pltpu.SemaphoreType.DMA
    return pl.pallas_call(
        step_kernel,
        name="graph_step",
        out_shape=(
            jax.ShapeDtypeStruct((NB, TILE), BF16),
            jax.ShapeDtypeStruct((TILE, TILE), F32),
            jax.ShapeDtypeStruct((TILE, TILE), F32),
        ),
        in_specs=[vmem, vmem, vmem, vmem, pl.BlockSpec(memory_space=pl.ANY), vmem, vmem, vmem],
        out_specs=(vmem, vmem, vmem),
        scratch_shapes=[
            pltpu.VMEM((DEAD + 1, TILE, TILE), BF16),
            pltpu.VMEM((PLANE, TILE), jnp.int32),
            pltpu.SMEM((PLANE, TILE), jnp.int32),
            pltpu.VMEM((PLANE, NB, TILE), BF16),
            pltpu.VMEM((PLANE, NB, TILE), BF16),
            pltpu.VMEM((PLANE, NB, TILE), BF16),
            pltpu.VMEM((TILE, TILE), BF16),
            pltpu.VMEM((TILE, TILE), BF16),
            pltpu.VMEM((NB, TILE), F32),
            pltpu.VMEM((NB, TILE), F32),
            pltpu.VMEM((NB, TILE), F32),
            pltpu.VMEM((NB, TILE), BF16),
            pltpu.VMEM((NB, TILE), BF16),
            pltpu.VMEM((NB, TILE), BF16),
            pltpu.VMEM((3, TILE, TILE), BF16),
            pltpu.VMEM((3, TILE, TILE), BF16),
            pltpu.VMEM((3, TILE, TILE), BF16),
            pltpu.VMEM((TILE, TILE), BF16),
            pltpu.VMEM((TILE, TILE), F32),
            pltpu.VMEM((NB, TILE), BF16),
            pltpu.VMEM((PLANE, 16, TILE), F32),
            pltpu.VMEM((PLANE, 16, TILE), F32),
            pltpu.VMEM((PLANE, 16, TILE), F32),
            pltpu.VMEM((16, TILE), F32),
            pltpu.VMEM((PLANE, 16, TILE), F32),
            dma((2,)),
            dma((3, 4)),
            dma((3, 4)),
            dma((3, 15)),
            dma((3, 15)),
            dma((3, 15)),
            dma((3, 15)),
            dma((3, 3)),
            dma((3, 3)),
            dma((3,)),
            dma((3,)),
            dma((3, 16)),
            dma((3, 16)),
        ],
        compiler_params=pltpu.CompilerParams(
            collective_id=0, has_side_effects=True, vmem_limit_bytes=48 << 20
        ),
    )(
        features, weight_one, weight_two, cotangent,
        adj_tiles.reshape(DEAD, TILE, TILE),
        tile_rows.reshape(PLANE, 16), tile_cols.reshape(PLANE, 16), tile_counts,
    )


def solution(mesh):
    placed = (
        P("row", None),
        P(),
        P(),
        P("row", None),
        P("row", "rep", None, None, None),
        P("row", "rep", None),
        P("row", "rep", None),
        P("row", "rep"),
    )
    return jax.shard_map(
        per_device,
        mesh=mesh,
        in_specs=placed,
        out_specs=(P("row", None), P(), P()),
        check_vma=False,
    )
```

time: 1370 us -> 95.8 us (0.07); the launches traced: 1350 us -> 95.4 us
  waiting for transfers between devices: 809 us -> 0 us
  local copies, waits for them, and re-layouts: 259 us -> 7.28 us
  matrix products: 141 us -> 0 us
  Pallas kernels: 0 us -> 87.5 us
  other arithmetic: 80.6 us -> 0 us
  blocking collectives: 39.7 us -> 0 us
    psum x2 -> x0, waiting for transfers between devices: 628 us -> none  [the longest x1 628 us: per_device(): grad_one = lax.psum(row_contract(s_one, d_pre), 'row')]
    all_gather x3 -> x0, waiting for transfers between devices: 180 us -> none  [propagate(): piece = lax.all_gather(own_block, 'row', axis=0, tiled=True)]
    dot_general x101 -> x0, matrix products: 141 us -> none  [the longest x48 68.1 us: section_work(): jnp.einsum('mij,mjf->mif', section_tiles, sources, preferred_element_type...]
    dynamic_update_slice x3 -> x0, local copies, waits for them, and re-layouts: 117 us -> none  [propagate(): widened = lax.dynamic_update_slice_in_dim(widened, piece, offset, 0)]
    pallas_call x0 -> x1, Pallas kernels: none -> 87.5 us  [per_device(): pl.pallas_call(step_kernel, name='graph_step', out_shape=(jax.ShapeDtypeS...]
    psum x2 -> x0, blocking collectives: 39.7 us -> none  [whole_sum(): return lax.psum(partial_rows, 'rep')]
    eq x48 -> x0, local copies, waits for them, and re-layouts: 33.5 us -> none  [section_work(): section_rows[:, None] == jnp.arange(count_tiles, dtype=jnp.int32)[None, :]]
    and x48 -> x0, other arithmetic: 33.4 us -> none  [section_work(): sources = jnp.take(pieces, section_cols, axis=0)]
  transfers between devices with their start and end apart: 5 -> 0, of which waited for: 3 -> 0; matrix products, arithmetic and copies ran while one was open for 25% -> 0% of each run, Pallas kernels for 0% -> 0%
where the time goes in v1:
time: 95.8 us; the launch traced here: 95.4 us
  Pallas kernels  87.5 us (91%)
  local copies, waits for them, and re-layouts  7.28 us (8%)
    pallas_call x1, Pallas kernels, per_device(): pl.pallas_call(step_kernel, name='graph_step', out_shape=(jax.ShapeDtypeS...  87.5 us
    unnamed x17, local copies, waits for them, and re-layouts  7.28 us

profile of v1, /device:TPU:1, one launch (start us, length us, event | category | flops | bytes accessed | tf_op | source)
XLA Modules:
  0.0 95.4 jit_solution(2609066299078520579)
XLA Ops:
  0.6 0.0 copy-start
  0.6 0.9 copy-done
  1.5 0.0 copy-start.1
  1.5 0.9 copy-done.1
  2.4 0.0 copy-start.2
  2.4 0.8 copy-done.2
  3.2 0.0 copy-start.3
  3.2 0.8 copy-done.3
  4.0 0.0 copy-start.4
  4.0 0.7 copy-done.4
  4.7 0.0 copy-start.5
  4.7 0.7 copy-done.5
  5.4 0.0 copy-start.6
  5.4 0.7 copy-done.6
  6.0 87.5 %graph_step.1 = (bf16[512,128]{1,0:T(8,128)(2,1)S(1)}, f32[128,128]{1,0:T(8,128)S(1)}, f32[128,128]{1,0:T(8,128)S(1)}) custom-call(bf16[512,128]{1,0:T(8,128)(2,1)S(1)} %copy-done, bf16[128,128]{1,0:T(8,128)(2,1)S(1)} %copy-done.2, bf16[128,128]{1,0:T(8,128)(2,1)S(1)} %copy-done.3, bf16[512,128]{1,0:T(8,128)(2,1)S(1)} %copy-done.1, ...), custom_call_target="tpu_custom_call" | custom-call | tf_op jit(solution)/shard_map/graph_step/pallas_call | solution.py:398
  93.5 0.7 copy.14
  94.2 0.6 copy.15
  94.8 0.6 copy.16
Async XLA Ops:
  0.6 0.9 copy-start
  1.5 0.9 copy-start.1
  2.4 0.8 copy-start.2
  3.2 0.8 copy-start.3
  4.0 0.7 copy-start.4
  4.7 0.7 copy-start.5
  5.4 0.7 copy-start.6

commit v2 on v1

--- a/solution.py
+++ b/solution.py
@@ -32,9 +32,9 @@
 
 
 def step_kernel(
-    feat, w_one, w_two, cot, adj, rows_in, cols_in, counts_in,
+    feat, w_one_in, w_two_in, cot_in, adj, rows_hbm, cols_hbm, counts_hbm,
     out, grad_one, grad_two,
-    tiles, table_v, table_s, xf, xd, xh, dq, hq, acc_f, acc_d, acc_h,
+    w_one, w_two, cot, rows_in, cols_in, counts_in, tiles, table_v, table_s, xf, xd, xh, dq, hq, acc_f, acc_d, acc_h,
     part_f, part_d, part_h, red_f, red_d, red_h, s_one_q, slope_q, out_buf,
     gpart, grs, gcol, gred, gall,
     local_sem, z_send, z_recv, a_send, a_recv, b_send, b_recv,
@@ -48,8 +48,6 @@
     x = lax.rem(place, SIDE)
     column = zh * REPS + rep
 
-    adj_copy = pltpu.make_async_copy(adj, tiles.at[pl.ds(0, DEAD)], local_sem.at[0])
-    adj_copy.start()
 
     def plane_peer(step):
         return (zh * PLANE + wrap(place + step, PLANE), rep)
@@ -73,15 +71,31 @@
             device_id=peer, device_id_type=MESH,
         )
 
+    def local(src, dst, at):
+        return pltpu.make_async_copy(src, dst, local_sem.at[at])
+
     barrier = pltpu.get_barrier_semaphore()
 
-    def greet(step, carry):
-        pl.semaphore_signal(barrier, inc=1, device_id=plane_peer(step), device_id_type=MESH)
-        pl.semaphore_signal(barrier, inc=1, device_id=column_peer(step), device_id_type=MESH)
-        return carry
-
-    lax.fori_loop(1, PLANE, greet, 0)
-    pl.semaphore_wait(barrier, 2 * (PLANE - 1))
+    def greet(peer):
+        pl.semaphore_signal(barrier, inc=1, device_id=peer, device_id_type=MESH)
+
+    for q in range(REPS):
+        @pl.when(jnp.logical_or(rep != zh, rep != q))
+        def _(q=q):
+            greet((rep * PLANE + place, q))
+
+    for step in (2, 1, 3):
+        greet(x_peer(step))
+        greet(y_peer(step))
+        greet(rep_peer(step))
+    loads = [
+        local(cot_in, cot, 0), local(w_two_in, w_two, 1), local(counts_hbm, counts_in, 2),
+        local(rows_hbm, rows_in, 3), local(cols_hbm, cols_in, 4), local(w_one_in, w_one, 5),
+        local(adj, tiles.at[pl.ds(0, DEAD)], 6),
+    ]
+    for load in loads:
+        load.start()
+    pl.semaphore_wait(barrier, 13 - jnp.where(rep == zh, 1, 0))
 
     def z_copy(t, buf, src, step):
         return remote(
@@ -91,8 +105,11 @@
             (wrap(zh + step, REPS) * PLANE + place, zh),
         )
 
+    def own_copy(t, buf, src):
+        return local(src, buf.at[place, pl.ds(pl.multiple_of(rep * TILE, TILE), TILE)], 8 + t)
+
     def z_start(t, buf, src):
-        for step in (1, 2, 3):
+        for step in (2, 1, 3):
             z_copy(t, buf, src, step).start()
 
         @pl.when(rep != zh)
@@ -101,7 +118,7 @@
 
         @pl.when(rep == zh)
         def _():
-            buf[place, pl.ds(pl.multiple_of(rep * TILE, TILE), TILE)] = src[...]
+            own_copy(t, buf, src).start()
 
     def z_finish(t, buf, src):
         for step in (1, 2, 3):
@@ -118,6 +135,10 @@
                 src, buf.at[place, pl.ds(quarter * TILE, TILE)],
                 z_send.at[t, 0], z_recv.at[t, quarter], rep_peer(1),
             ).wait_recv()
+
+        @pl.when(jnp.logical_and(rep == zh, rep == quarter))
+        def _():
+            own_copy(t, buf, src).wait()
 
     def a_block(dy, dx):
         return wrap(y - dy, SIDE) * SIDE + wrap(x - dx, SIDE)
@@ -242,11 +263,16 @@
 
     fq = feat.at[quarter]
     z_start(0, xf, fq)
+    loads[0].wait()
+    loads[1].wait()
     dq[...] = lax.dot_general(
         cot[quarter], w_two[...], (((1,), (1,)), ((), ())), preferred_element_type=F32
     ).astype(BF16)
     z_start(1, xd, dq)
 
+    loads[2].wait()
+    loads[3].wait()
+    loads[4].wait()
     lanes = lax.broadcasted_iota(jnp.int32, (PLANE, TILE), 1)
     sections = lax.broadcasted_iota(jnp.int32, (PLANE, TILE), 0)
     small_lane = lax.broadcasted_iota(jnp.int32, (PLANE, PLANE), 1)
@@ -260,7 +286,7 @@
     for slot in range(16):
         table = jnp.where(cell[:, slot : slot + 1] == lanes, sections * 16 + slot, table)
     table_v[...] = table
-    table_copy = pltpu.make_async_copy(table_v, table_s, local_sem.at[1])
+    table_copy = local(table_v, table_s, 7)
     table_copy.start()
     tiles[DEAD] = jnp.zeros((TILE, TILE), BF16)
     acc_f[...] = jnp.zeros_like(acc_f)
@@ -269,7 +295,8 @@
 
     spread_start(0, xf, fq)
     table_copy.wait()
-    adj_copy.wait()
+    loads[5].wait()
+    loads[6].wait()
     spread_forward(0, xf)
     consume_near(xf, acc_f)
     spread_start(1, xd, dq)
@@ -403,9 +430,15 @@
             jax.ShapeDtypeStruct((TILE, TILE), F32),
             jax.ShapeDtypeStruct((TILE, TILE), F32),
         ),
-        in_specs=[vmem, vmem, vmem, vmem, pl.BlockSpec(memory_space=pl.ANY), vmem, vmem, vmem],
+        in_specs=[pl.BlockSpec(memory_space=pltpu.HBM)] * 8,
         out_specs=(vmem, vmem, vmem),
         scratch_shapes=[
+            pltpu.VMEM((TILE, TILE), BF16),
+            pltpu.VMEM((TILE, TILE), BF16),
+            pltpu.VMEM((NB, TILE), BF16),
+            pltpu.VMEM((PLANE, 16), jnp.int32),
+            pltpu.VMEM((PLANE, 16), jnp.int32),
+            pltpu.VMEM((1, 16), jnp.int32),
             pltpu.VMEM((DEAD + 1, TILE, TILE), BF16),
             pltpu.VMEM((PLANE, TILE), jnp.int32),
             pltpu.SMEM((PLANE, TILE), jnp.int32),
@@ -431,7 +464,7 @@
             pltpu.VMEM((PLANE, 16, TILE), F32),
             pltpu.VMEM((16, TILE), F32),
             pltpu.VMEM((PLANE, 16, TILE), F32),
-            dma((2,)),
+            dma((11,)),
             dma((3, 4)),
             dma((3, 4)),
             dma((3, 15)),
@@ -446,7 +479,7 @@
             dma((3, 16)),
         ],
         compiler_params=pltpu.CompilerParams(
-            collective_id=0, has_side_effects=True, vmem_limit_bytes=48 << 20
+            collective_id=0, has_side_effects=True, vmem_limit_bytes=64 << 20
         ),
     )(
         features, weight_one, weight_two, cotangent,

time: 95.8 us -> 93.2 us (0.973)
  local copies, waits for them, and re-layouts: 7.28 us -> 4.51 us
    unnamed x17 -> x3, local copies, waits for them, and re-layouts: 7.28 us -> 4.51 us
where the time goes in v2:
time: 93.2 us; the launch traced here: 93 us
  Pallas kernels  87.8 us (94%)
  local copies, waits for them, and re-layouts  4.51 us (5%)
    pallas_call x1, Pallas kernels, per_device(): pl.pallas_call(step_kernel, name='graph_step', out_shape=(jax.ShapeDtypeS...  87.8 us
    unnamed x3, local copies, waits for them, and re-layouts  4.51 us

profile of v2, /device:TPU:1, one launch (start us, length us, event | category | flops | bytes accessed | tf_op | source)
XLA Modules:
  0.0 93.0 jit_solution(11244714280268395739)
XLA Ops:
  0.6 87.8 %graph_step.1 = (bf16[512,128]{1,0:T(8,128)(2,1)}, f32[128,128]{1,0:T(8,128)}, f32[128,128]{1,0:T(8,128)}) custom-call(bf16[512,128]{1,0:T(8,128)(2,1)} %feat.1, bf16[128,128]{1,0:T(8,128)(2,1)} %w_one_in.1, bf16[128,128]{1,0:T(8,128)(2,1)} %w_two_in.1, bf16[512,128]{1,0:T(8,128)(2,1)} %cot_in.1, bf16[256,128,128]{2,1,0:T(8,128)(2,1)} %bitcast.3, ...), custom_call_target="tpu_custom_call" | custom-call | tf_op jit(solution)/shard_map/graph_step/pallas_call | solution.py:425
  88.5 1.6 %copy.14 = bf16[512,128]{1,0:T(8,128)(2,1)} copy(bf16[512,128]{1,0:T(8,128)(2,1)} %get-tuple-element.6) | data formatting | bytes 262144
  90.0 1.5 %copy.15 = f32[128,128]{1,0:T(8,128)} copy(f32[128,128]{1,0:T(8,128)} %get-tuple-element.7) | data formatting | bytes 131072
  91.5 1.5 %copy.16 = f32[128,128]{1,0:T(8,128)} copy(f32[128,128]{1,0:T(8,128)} %get-tuple-element.8) | data formatting | bytes 131072

commit v3 on v2

--- a/solution.py
+++ b/solution.py
@@ -15,6 +15,7 @@
 DEAD = 256
 BF16 = jnp.bfloat16
 F32 = jnp.float32
+GSUM = jnp.float32
 
 
 def gelu_parts(values):
@@ -33,7 +34,7 @@
 
 def step_kernel(
     feat, w_one_in, w_two_in, cot_in, adj, rows_hbm, cols_hbm, counts_hbm,
-    out, grad_one, grad_two,
+    out, grads,
     w_one, w_two, cot, rows_in, cols_in, counts_in, tiles, table_v, table_s, xf, xd, xh, dq, hq, acc_f, acc_d, acc_h,
     part_f, part_d, part_h, red_f, red_d, red_h, s_one_q, slope_q, out_buf,
     gpart, grs, gcol, gred, gall,
@@ -50,11 +51,13 @@
 
 
     def plane_peer(step):
-        return (zh * PLANE + wrap(place + step, PLANE), rep)
+        dy, dx = step // SIDE, lax.rem(step, SIDE)
+        return (zh * PLANE + wrap(y + dy, SIDE) * SIDE + wrap(x + dx, SIDE), rep)
 
     def column_peer(step):
-        other = wrap(column + step, PLANE)
-        return ((other // REPS) * PLANE + place, lax.rem(other, REPS))
+        dz, dc = step // 2, lax.rem(step, 2)
+        z = lax.rem(2 * zh + rep // 2 + dz, 2 * REPS)
+        return ((z // 2) * PLANE + place, lax.rem(z, 2) * 2 + lax.rem(rep + dc, 2))
 
     def rep_peer(step):
         return (row, wrap(rep + step, REPS))
@@ -206,39 +209,36 @@
 
         lax.fori_loop(0, 3, body, 0)
 
-    def consume(buf, acc, block, half):
-        right = buf[block, pl.ds(half * HALF, HALF)]
+    def multiply(acc, blocks, half, rights):
+        right = jnp.concatenate(rights, axis=0)
         for k in range(4):
             left = jnp.concatenate(
-                [tiles[table_s[block, 4 * k + 2 * half]], tiles[table_s[block, 4 * k + 2 * half + 1]]],
+                [tiles[table_s[block, 4 * k + 2 * half + c]] for block in blocks for c in range(2)],
                 axis=1,
             )
             acc[pl.ds(k * TILE, TILE)] += jnp.dot(left, right, preferred_element_type=F32)
 
+    def consume(buf, acc, blocks, half):
+        multiply(acc, blocks, half, [buf[block, pl.ds(half * HALF, HALF)] for block in blocks])
+
     def consume_near(buf, acc):
-        def body(i, carry):
-            away = ring_step(i)
-            consume(buf, acc, a_block(0, away), 0)
-            consume(buf, acc, a_block(away, 0), 1)
+        consume(buf, acc, [a_block(0, ring_step(i)) for i in range(4)], 0)
+        consume(buf, acc, [a_block(ring_step(i), 0) for i in range(4)], 1)
+
+    def consume_far(t, buf, acc, start, stop):
+        def body(j, carry):
+            e = ring_step(j + 1)
+            blocks = [a_block(e, ring_step(i)) for i in range(4)]
+            for i in range(4):
+                second_a(t, buf, j, i, blocks[i]).wait_recv()
+            consume(buf, acc, blocks, 0)
+            blocks = [a_block(ring_step(i), e) for i in range(4)]
+            for i in range(4):
+                second_b(t, buf, j, i, blocks[i]).wait_recv()
+            consume(buf, acc, blocks, 1)
             return carry
 
-        lax.fori_loop(0, 4, body, 0)
-
-    def consume_far(t, buf, acc, start, stop):
-        def body(n, carry):
-            j = n // 4
-            i = lax.rem(n, 4)
-            e = ring_step(j + 1)
-            d = ring_step(i)
-            block = a_block(e, d)
-            second_a(t, buf, j, i, block).wait_recv()
-            consume(buf, acc, block, 0)
-            block = a_block(d, e)
-            second_b(t, buf, j, i, block).wait_recv()
-            consume(buf, acc, block, 1)
-            return carry
-
-        lax.fori_loop(start, stop, body, 0)
+        lax.fori_loop(start // 4, stop // 4, body, 0)
 
     def rep_copy(t, part, red, step):
         return remote(
@@ -268,7 +268,6 @@
     dq[...] = lax.dot_general(
         cot[quarter], w_two[...], (((1,), (1,)), ((), ())), preferred_element_type=F32
     ).astype(BF16)
-    z_start(1, xd, dq)
 
     loads[2].wait()
     loads[3].wait()
@@ -294,6 +293,7 @@
     acc_h[...] = jnp.zeros_like(acc_h)
 
     spread_start(0, xf, fq)
+    z_start(1, xd, dq)
     table_copy.wait()
     loads[5].wait()
     loads[6].wait()
@@ -321,18 +321,18 @@
     g_one = lax.dot_general(
         s_one_q[...], d_pre, (((0,), (0,)), ((), ())), preferred_element_type=F32
     )
-    gpart[:, 0:8, :] = g_one.reshape(PLANE, 8, TILE)
+    gpart[:, 0:8, :] = g_one.reshape(PLANE, 8, TILE).astype(GSUM)
     consume_far(2, xh, acc_h, 0, 12)
     rep_start(2, acc_h, part_h, red_h)
 
     g_two = lax.dot_general(
         part_h[...], cot[...], (((0,), (0,)), ((), ())), preferred_element_type=F32
     )
-    gpart[:, 8:16, :] = g_two.reshape(PLANE, 8, TILE)
+    gpart[:, 8:16, :] = g_two.reshape(PLANE, 8, TILE).astype(GSUM)
 
     def plane_sum(step):
         return remote(
-            gpart.at[wrap(place + step, PLANE)], grs.at[step],
+            gpart.at[lax.rem(plane_peer(step)[0], PLANE)], grs.at[step],
             g_send.at[0, step], g_recv.at[0, step], plane_peer(step),
         )
 
@@ -348,19 +348,16 @@
             g_send.at[2, step], g_recv.at[2, step], plane_peer(step),
         )
 
-    def start_all(make):
-        def body(step, carry):
+    far_plane = (10, 6, 9, 11, 14, 2, 5, 7, 8, 13, 15, 1, 3, 4, 12)
+    far_column = (8, 9, 6, 7, 10, 11, 4, 5, 12, 13, 2, 3, 14, 15, 1)
+
+    def start_all(make, order):
+        for step in order:
             make(step).start()
-            return carry
-
-        lax.fori_loop(1, PLANE, body, 0)
 
     def receive_all(make):
-        def body(step, carry):
+        for step in range(1, PLANE):
             make(step).wait_recv()
-            return carry
-
-        lax.fori_loop(1, PLANE, body, 0)
 
     def sent_all(make):
         def body(step, carry):
@@ -369,7 +366,7 @@
 
         lax.fori_loop(1, PLANE, body, 0)
 
-    start_all(plane_sum)
+    start_all(plane_sum, far_plane)
 
     s_two = rep_sum(2, acc_h, part_h, red_h).astype(BF16)
     out_buf[quarter] = jnp.dot(s_two, w_two[...], preferred_element_type=F32).astype(BF16)
@@ -384,25 +381,24 @@
         out_copy(step).start()
 
     receive_all(plane_sum)
-    mine = gpart[place]
+    mine = gpart[place].astype(F32)
     for step in range(1, PLANE):
-        mine = mine + grs[step]
-    gcol[column] = mine
-    start_all(column_share)
+        mine = mine + grs[step].astype(F32)
+    gcol[column] = mine.astype(GSUM)
+    start_all(column_share, far_column)
     receive_all(column_share)
-    mine = gcol[0]
+    mine = gcol[0].astype(F32)
     for other in range(1, PLANE):
-        mine = mine + gcol[other]
+        mine = mine + gcol[other].astype(F32)
     gred[...] = mine
-    start_all(plane_gather)
+    start_all(plane_gather, far_plane)
     gall[place] = mine
 
     for step in (1, 2, 3):
         out_copy(step).wait_recv()
     out[...] = out_buf[...]
     receive_all(plane_gather)
-    grad_one[...] = gall[:, 0:8, :].reshape(TILE, TILE)
-    grad_two[...] = gall[:, 8:16, :].reshape(TILE, TILE)
+    grads[...] = gall[...]
 
     for t, buf, src in ((0, xf, fq), (1, xd, dq), (2, xh, hq)):
         z_finish(t, buf, src)
@@ -422,16 +418,15 @@
 ):
     vmem = pl.BlockSpec(memory_space=pltpu.VMEM)
     dma = pltpu.SemaphoreType.DMA
-    return pl.pallas_call(
+    output, grads = pl.pallas_call(
         step_kernel,
         name="graph_step",
         out_shape=(
             jax.ShapeDtypeStruct((NB, TILE), BF16),
-            jax.ShapeDtypeStruct((TILE, TILE), F32),
-            jax.ShapeDtypeStruct((TILE, TILE), F32),
+            jax.ShapeDtypeStruct((PLANE, 16, TILE), F32),
         ),
         in_specs=[pl.BlockSpec(memory_space=pltpu.HBM)] * 8,
-        out_specs=(vmem, vmem, vmem),
+        out_specs=(vmem, vmem),
         scratch_shapes=[
             pltpu.VMEM((TILE, TILE), BF16),
             pltpu.VMEM((TILE, TILE), BF16),
@@ -459,9 +454,9 @@
             pltpu.VMEM((TILE, TILE), BF16),
             pltpu.VMEM((TILE, TILE), F32),
             pltpu.VMEM((NB, TILE), BF16),
-            pltpu.VMEM((PLANE, 16, TILE), F32),
-            pltpu.VMEM((PLANE, 16, TILE), F32),
-            pltpu.VMEM((PLANE, 16, TILE), F32),
+            pltpu.VMEM((PLANE, 16, TILE), GSUM),
+            pltpu.VMEM((PLANE, 16, TILE), GSUM),
+            pltpu.VMEM((PLANE, 16, TILE), GSUM),
             pltpu.VMEM((16, TILE), F32),
             pltpu.VMEM((PLANE, 16, TILE), F32),
             dma((11,)),
@@ -486,6 +481,11 @@
         adj_tiles.reshape(DEAD, TILE, TILE),
         tile_rows.reshape(PLANE, 16), tile_cols.reshape(PLANE, 16), tile_counts,
     )
+    return (
+        output,
+        grads[:, 0:8, :].reshape(TILE, TILE),
+        grads[:, 8:16, :].reshape(TILE, TILE),
+    )
 
 
 def solution(mesh):

time: 93.2 us -> 85.2 us (0.914)
  Pallas kernels: 87.8 us -> 81.2 us
  local copies, waits for them, and re-layouts: 4.51 us -> 3.1 us
    pallas_call x1, Pallas kernels: 87.8 us -> 81.2 us  [per_device(): pl.pallas_call(step_kernel, name='graph_step', out_shape=(jax.ShapeDtypeS...]
    unnamed x3 -> x1, local copies, waits for them, and re-layouts: 4.51 us -> 1.57 us
    reshape x0 -> x1, local copies, waits for them, and re-layouts: none -> 1.53 us  [per_device(): grads[:, 8:16, :].reshape(TILE, TILE)]
where the time goes in v3:
time: 85.2 us; the launch traced here: 85 us
  Pallas kernels  81.2 us (95%)
  local copies, waits for them, and re-layouts  3.1 us (4%)
    pallas_call x1, Pallas kernels, per_device(): pl.pallas_call(step_kernel, name='graph_step', out_shape=(jax.ShapeDtypeS...  81.2 us

profile of v3, /device:TPU:1, one launch (start us, length us, event | category | flops | bytes accessed | tf_op | source)
XLA Modules:
  0.0 85.0 jit_solution(18156163526237033519)
XLA Ops:
  0.6 81.2 %graph_step.1 = (bf16[512,128]{1,0:T(8,128)(2,1)}, f32[16,16,128]{2,1,0:T(8,128)}) custom-call(bf16[512,128]{1,0:T(8,128)(2,1)} %feat.1, bf16[128,128]{1,0:T(8,128)(2,1)} %w_one_in.1, bf16[128,128]{1,0:T(8,128)(2,1)} %w_two_in.1, bf16[512,128]{1,0:T(8,128)(2,1)} %cot_in.1, bf16[256,128,128]{2,1,0:T(8,128)(2,1)} %bitcast.7, s32[16,16]{1,0:T(8,128)} %bitcast.8, ...), custom_call_target="tpu_custom_call" | custom-call | tf_op jit(solution)/shard_map/graph_step/pallas_call | solution.py:421
  81.9 1.5 %slice_bitcast_fusion = (f32[128,128]{1,0:T(8,128)}, f32[128,128]{1,0:T(8,128)}) fusion(f32[16,16,128]{2,1,0:T(8,128)} %get-tuple-element.6), kind=kLoop, calls=%fused_computation | loop fusion | bytes 262144 | tf_op jit(solution)/shard_map/reshape | solution.py:487
  83.4 1.6 %copy.12 = bf16[512,128]{1,0:T(8,128)(2,1)} copy(bf16[512,128]{1,0:T(8,128)(2,1)} %get-tuple-element.12) | data formatting | bytes 262144

commit v4 on v3

--- a/solution.py
+++ b/solution.py
@@ -293,11 +293,11 @@
     acc_h[...] = jnp.zeros_like(acc_h)
 
     spread_start(0, xf, fq)
-    z_start(1, xd, dq)
     table_copy.wait()
     loads[5].wait()
     loads[6].wait()
     spread_forward(0, xf)
+    z_start(1, xd, dq)
     consume_near(xf, acc_f)
     spread_start(1, xd, dq)
     consume_far(0, xf, acc_f, 0, 12)
@@ -311,6 +311,8 @@
     z_start(2, xh, hq)
     s_one_q[...] = s_one
     slope_q[...] = slope
+    z_finish(0, xf, fq)
+    spread_finish(0, xf)
     consume_near(xd, acc_d)
     spread_start(2, xh, hq)
     consume_far(1, xd, acc_d, 0, 12)
@@ -380,12 +382,22 @@
     for step in (2, 3, 1):
         out_copy(step).start()
 
+    z_finish(1, xd, dq)
+    spread_finish(1, xd)
+    for t, part, red in ((0, part_f, red_f), (1, part_d, red_d)):
+        for step in (1, 2, 3):
+            rep_copy(t, part, red, step).wait_send()
     receive_all(plane_sum)
     mine = gpart[place].astype(F32)
     for step in range(1, PLANE):
         mine = mine + grs[step].astype(F32)
     gcol[column] = mine.astype(GSUM)
     start_all(column_share, far_column)
+    z_finish(2, xh, hq)
+    spread_finish(2, xh)
+    for step in (1, 2, 3):
+        rep_copy(2, part_h, red_h, step).wait_send()
+    sent_all(plane_sum)
     receive_all(column_share)
     mine = gcol[0].astype(F32)
     for other in range(1, PLANE):
@@ -397,19 +409,12 @@
     for step in (1, 2, 3):
         out_copy(step).wait_recv()
     out[...] = out_buf[...]
+    for step in (1, 2, 3):
+        out_copy(step).wait_send()
+    sent_all(column_share)
     receive_all(plane_gather)
     grads[...] = gall[...]
 
-    for t, buf, src in ((0, xf, fq), (1, xd, dq), (2, xh, hq)):
-        z_finish(t, buf, src)
-        spread_finish(t, buf)
-    for t, part, red in ((0, part_f, red_f), (1, part_d, red_d), (2, part_h, red_h)):
-        for step in (1, 2, 3):
-            rep_copy(t, part, red, step).wait_send()
-    for step in (1, 2, 3):
-        out_copy(step).wait_send()
-    sent_all(plane_sum)
-    sent_all(column_share)
     sent_all(plane_gather)
 
 

time: 85.2 us -> 84.4 us (level)
  no operation moved by 1% of the time
where the time goes in v4:
time: 84.4 us; the launch traced here: 84.2 us
  Pallas kernels  80.4 us (95%)
  local copies, waits for them, and re-layouts  3.1 us (4%)
    pallas_call x1, Pallas kernels, per_device(): pl.pallas_call(step_kernel, name='graph_step', out_shape=(jax.ShapeDtypeS...  80.4 us

profile of v4, /device:TPU:1, one launch (start us, length us, event | category | flops | bytes accessed | tf_op | source)
XLA Modules:
  0.0 84.2 jit_solution(14502011551151034783)
XLA Ops:
  0.6 80.4 %graph_step.1 = (bf16[512,128]{1,0:T(8,128)(2,1)}, f32[16,16,128]{2,1,0:T(8,128)}) custom-call(bf16[512,128]{1,0:T(8,128)(2,1)} %feat.1, bf16[128,128]{1,0:T(8,128)(2,1)} %w_one_in.1, bf16[128,128]{1,0:T(8,128)(2,1)} %w_two_in.1, bf16[512,128]{1,0:T(8,128)(2,1)} %cot_in.1, bf16[256,128,128]{2,1,0:T(8,128)(2,1)} %bitcast.7, s32[16,16]{1,0:T(8,128)} %bitcast.8, ...), custom_call_target="tpu_custom_call" | custom-call | tf_op jit(solution)/shard_map/graph_step/pallas_call | solution.py:426
  81.1 1.5 %slice_bitcast_fusion = (f32[128,128]{1,0:T(8,128)}, f32[128,128]{1,0:T(8,128)}) fusion(f32[16,16,128]{2,1,0:T(8,128)} %get-tuple-element.6), kind=kLoop, calls=%fused_computation | loop fusion | bytes 262144 | tf_op jit(solution)/shard_map/reshape | solution.py:492
  82.6 1.6 %copy.12 = bf16[512,128]{1,0:T(8,128)(2,1)} copy(bf16[512,128]{1,0:T(8,128)(2,1)} %get-tuple-element.12) | data formatting | bytes 262144

commit v5 on v4

--- a/solution.py
+++ b/solution.py
@@ -15,7 +15,7 @@
 DEAD = 256
 BF16 = jnp.bfloat16
 F32 = jnp.float32
-GSUM = jnp.float32
+GSUM = jnp.bfloat16
 
 
 def gelu_parts(values):

time: 84.4 us -> 84.2 us (level)
  no operation moved by 1% of the time
where the time goes in v5:
time: 84.2 us; the launch traced here: 84 us
  Pallas kernels  80.3 us (95%)
  local copies, waits for them, and re-layouts  3.1 us (4%)
    pallas_call x1, Pallas kernels, per_device(): pl.pallas_call(step_kernel, name='graph_step', out_shape=(jax.ShapeDtypeS...  80.3 us

profile of v5, /device:TPU:1, one launch (start us, length us, event | category | flops | bytes accessed | tf_op | source)
XLA Modules:
  0.0 84.0 jit_solution(10174494585500176728)
XLA Ops:
  0.6 80.3 %graph_step.1 = (bf16[512,128]{1,0:T(8,128)(2,1)}, f32[16,16,128]{2,1,0:T(8,128)}) custom-call(bf16[512,128]{1,0:T(8,128)(2,1)} %feat.1, bf16[128,128]{1,0:T(8,128)(2,1)} %w_one_in.1, bf16[128,128]{1,0:T(8,128)(2,1)} %w_two_in.1, bf16[512,128]{1,0:T(8,128)(2,1)} %cot_in.1, bf16[256,128,128]{2,1,0:T(8,128)(2,1)} %bitcast.7, s32[16,16]{1,0:T(8,128)} %bitcast.8, ...), custom_call_target="tpu_custom_call" | custom-call | tf_op jit(solution)/shard_map/graph_step/pallas_call | solution.py:426
  80.9 1.5 %slice_bitcast_fusion = (f32[128,128]{1,0:T(8,128)}, f32[128,128]{1,0:T(8,128)}) fusion(f32[16,16,128]{2,1,0:T(8,128)} %get-tuple-element.6), kind=kLoop, calls=%fused_computation | loop fusion | bytes 262144 | tf_op jit(solution)/shard_map/reshape | solution.py:492
  82.4 1.6 %copy.12 = bf16[512,128]{1,0:T(8,128)(2,1)} copy(bf16[512,128]{1,0:T(8,128)(2,1)} %get-tuple-element.12) | data formatting | bytes 262144
